TPU v7x, 32 devices: a whole 2x2x4 slice. The times are simulated.
32 devices in a mesh: enc: 8 (over y, x, core), dec: 4 (over z).
Axes of the slice: x: 2, y: 2, z: 4, core: 2. Of those that a mesh axis runs over, the one named last changes fastest.
Arguments:
- queries: bfloat16 [2048, 4096], P('dec', 'enc'), may hold values from -16 to 16
- out_grad: bfloat16 [2048, 4096], P('dec', 'enc'), may hold values from -6 to 6
- memory_keys: bfloat16 [4096, 4096], P('enc'), may hold values from -6 to 6
- memory_values: bfloat16 [4096, 4096], P('enc'), may hold values from -6 to 6
- ref_blocks: int32 [2048, 8], P('dec'), may hold values from 0 to 31, as said below
- ref_counts: int32 [2048], P('dec'), may hold values from 1 to 8
Outputs:
- context: bfloat16 [2048, 4096], P('dec', 'enc')
- query_grad: bfloat16 [2048, 4096], P('dec', 'enc')
- key_grad: bfloat16 [4096, 4096], P('enc', 'dec')
- value_grad: bfloat16 [4096, 4096], P('enc', 'dec')
Inputs may be any that keep to these rules, and one draw needn't show every extreme that they name: `ref_blocks`: each row holds 8 different block numbers.
All inputs are finite; a program needn't handle non-finite values.
Results may differ from a plain program's by a relative error of at most 0.0092.
Values may be sent and summed in bfloat16 or wider, within the bound.
A program may use at most 192 MiB of HBM per device.

v0:
```python
import jax
import jax.numpy as jnp
from jax import lax
from jax.sharding import PartitionSpec as P

DH = 64
BLOCK = 128


NEGATIVE = -1e30


def merged(shard, axis, combine):
    everything = jax.tree.map(lambda part: lax.all_gather(part, axis), shard)
    first = jax.tree.map(lambda part: part[0], everything)

    def lap(k, so_far):
        return combine(so_far, jax.tree.map(lambda part: part[k], everything))

    return lax.fori_loop(1, lax.axis_size(axis), lap, first)


def visible_cells(ref_blocks, ref_counts, first_block, block_total):
    slot_ids = jnp.arange(ref_blocks.shape[1], dtype=jnp.int32)
    live_slot = slot_ids[None, :] < ref_counts[:, None]
    wanted = jnp.arange(block_total, dtype=jnp.int32) + first_block
    matches = (ref_blocks[:, :, None] == wanted[None, None, :]) & live_slot[:, :, None]
    chosen = jnp.any(matches, axis=1)
    widened = jnp.broadcast_to(chosen[:, :, None], (chosen.shape[0], block_total, BLOCK))
    return widened.reshape(chosen.shape[0], block_total * BLOCK)


def join_stats(first_pair, second_pair):
    row_max = jnp.maximum(first_pair[0], second_pair[0])
    row_total = first_pair[1] * jnp.exp(first_pair[0] - row_max) + second_pair[1] * jnp.exp(
        second_pair[0] - row_max
    )
    return (row_max, row_total)


def body(queries, out_grad, memory_keys, memory_values, ref_blocks, ref_counts):
    all_queries, all_grads = (
        lax.all_gather(queries, "enc", axis=1, tiled=True),
        lax.all_gather(out_grad, "enc", axis=1, tiled=True),
    )
    cell_count = memory_keys.shape[0]
    token_count = queries.shape[0]
    full_width = all_queries.shape[1]
    block_total = cell_count // BLOCK
    visible = visible_cells(
        ref_blocks, ref_counts, lax.axis_index("enc") * block_total, block_total
    )
    group_heads = 8
    group_width = group_heads * DH
    group_count = full_width // group_width

    def group_slice(source, group_index, row_count):
        column_start = group_index * group_width
        piece = lax.dynamic_slice_in_dim(source, column_start, group_width, 1)
        return piece.reshape(row_count, group_heads, DH)

    def group_scores(group_index):
        query_group = group_slice(all_queries, group_index, token_count)
        key_group = group_slice(memory_keys, group_index, cell_count)
        scores = jnp.einsum(
            "thd,chd->htc", query_group, key_group, preferred_element_type=jnp.float32
        )
        return jnp.where(visible[None], scores, NEGATIVE)

    def group_stats(group_index):
        scores = group_scores(group_index)
        row_max = jnp.max(scores, axis=2)
        row_total = jnp.sum(
            jnp.where(visible[None], jnp.exp(scores - row_max[:, :, None]), 0.0), axis=2
        )
        return (row_max, row_total)

    row_max, row_total = lax.map(group_stats, jnp.arange(group_count, dtype=jnp.int32))
    row_max, row_total = merged((row_max, row_total), "enc", join_stats)
    log_total = row_max + jnp.log(row_total)

    def group_weights(group_index):
        scores = group_scores(group_index)
        group_log = lax.dynamic_index_in_dim(log_total, group_index, 0, False)
        return jnp.exp(scores - group_log[:, :, None])

    def forward_group(group_index, context_acc):
        rounded_weights = group_weights(group_index).astype(jnp.bfloat16)
        value_group = group_slice(memory_values, group_index, cell_count)
        attended = jnp.einsum(
            "htc,chd->thd", rounded_weights, value_group, preferred_element_type=jnp.float32
        )
        return lax.dynamic_update_slice_in_dim(
            context_acc, attended.reshape(token_count, group_width), group_index * group_width, 1
        )

    context_part = lax.fori_loop(
        0, group_count, forward_group, jnp.zeros((token_count, full_width), jnp.float32)
    )
    context_sum = lax.psum_scatter(context_part, "enc", scatter_dimension=1, tiled=True)
    local_heads = queries.shape[1] // DH
    own_terms = jnp.sum(
        (out_grad.astype(jnp.float32) * context_sum).reshape(token_count, local_heads, DH), axis=2
    )
    row_terms = lax.all_gather(own_terms, "enc", axis=1, tiled=True)

    def backward_group(group_index, carry):
        query_acc, key_acc, value_acc = carry
        column_start = group_index * group_width
        soft_weights = group_weights(group_index)
        query_group = group_slice(all_queries, group_index, token_count)
        grad_group = group_slice(all_grads, group_index, token_count)
        key_group = group_slice(memory_keys, group_index, cell_count)
        value_group = group_slice(memory_values, group_index, cell_count)
        weight_grad = jnp.einsum(
            "thd,chd->htc", grad_group, value_group, preferred_element_type=jnp.float32
        )
        group_terms = lax.dynamic_slice_in_dim(row_terms, group_index * group_heads, group_heads, 1)
        score_grad = (soft_weights * (weight_grad - group_terms.T[:, :, None])).astype(jnp.bfloat16)
        query_term = jnp.einsum(
            "htc,chd->thd", score_grad, key_group, preferred_element_type=jnp.float32
        )
        key_term = jnp.einsum(
            "htc,thd->chd", score_grad, query_group, preferred_element_type=jnp.float32
        )
        value_term = jnp.einsum(
            "htc,thd->chd",
            soft_weights.astype(jnp.bfloat16),
            grad_group,
            preferred_element_type=jnp.float32,
        )
        query_acc = lax.dynamic_update_slice_in_dim(
            query_acc, query_term.reshape(token_count, group_width), column_start, 1
        )
        key_acc = lax.dynamic_update_slice_in_dim(
            key_acc, key_term.reshape(cell_count, group_width), column_start, 1
        )
        value_acc = lax.dynamic_update_slice_in_dim(
            value_acc, value_term.reshape(cell_count, group_width), column_start, 1
        )
        return (query_acc, key_acc, value_acc)

    start_state = (
        jnp.zeros((token_count, full_width), jnp.float32),
        jnp.zeros((cell_count, full_width), jnp.float32),
        jnp.zeros((cell_count, full_width), jnp.float32),
    )
    query_part, key_cells, value_cells = lax.fori_loop(0, group_count, backward_group, start_state)
    query_sum = lax.psum_scatter(query_part, "enc", scatter_dimension=1, tiled=True)
    key_grad, value_grad = (
        lax.psum_scatter(key_cells, "dec", scatter_dimension=1, tiled=True),
        lax.psum_scatter(value_cells, "dec", scatter_dimension=1, tiled=True),
    )
    return (
        context_sum.astype(jnp.bfloat16),
        query_sum.astype(jnp.bfloat16),
        key_grad.astype(jnp.bfloat16),
        value_grad.astype(jnp.bfloat16),
    )


def solution(mesh):
    in_specs = (
        P("dec", "enc"),
        P("dec", "enc"),
        P("enc", None),
        P("enc", None),
        P("dec", None),
        P("dec"),
    )
    out_specs = (P("dec", "enc"), P("dec", "enc"), P("enc", "dec"), P("enc", "dec"))
    return jax.shard_map(body, mesh=mesh, in_specs=in_specs, out_specs=out_specs, check_vma=False)
```

profile of v0, /device:TPU:0, one launch (start us, length us, event | category | flops | bytes accessed | tf_op | source)
XLA Modules:
  0.0 968.6 jit_solution(5158436623159651812)
XLA Ops:
  7.2 2.0 copy.51
  9.4 6.5 copy.54
  16.1 33.9 %all-gather.7.cloned.1.call-done = bf16[512,4096]{0,1:T(8,128)(2,1)} async-done(((bf16[512,512]{0,1:T(8,128)(2,1)}), bf16[512,4096]{0,1:T(8,128)(2,1)}) %all-gather.7.cloned.1.call-update) | async-done | bytes 4194320 | tf_op jit(solution)/shard_map/all_gather | solution.py:43
  49.9 58.0 %while.63 = (s32[]{:T(128)}, f32[8,8,512]{2,1,0:T(8,128)S(1)}, f32[8,8,512]{2,1,0:T(8,128)}, s32[8]{0:T(128)S(1)}, bf16[512,4096]{0,1:T(8,128)(2,1)}, /*index=5*...) while((s32[]{:T(128)}, f32[8,8,512]{2,1,0:T(8,128)S(1)}, ...), condition=%wide.region_4.5_spmd.clone, body=%wide.region_1.4_spmd.clone.sunk | while | flops 281010176 | bytes 20826300 | solution.py:78
  54.8 1.7 select_reduce_fusion.5
  109.6 6.5 copy.53
  116.1 16.2 %all-gather.11.cloned.1.call-done = f32[64,8,512]{2,1,0:T(8,128)} async-done(((f32[8,8,512]{2,1,0:T(8,128)}), f32[64,8,512]{2,1,0:T(8,128)}) %all-gather.11.cloned.1.call-update) | async-done | bytes 1048592 | tf_op jit(solution)/shard_map/all_gather | solution.py:14
  133.2 25.1 %all-gather.13.cloned.1.call-done = f32[64,8,512]{2,1,0:T(8,128)} async-done(((f32[8,8,512]{2,1,0:T(8,128)}), f32[64,8,512]{2,1,0:T(8,128)}) %all-gather.13.cloned.1.call-update) | async-done | bytes 1048592 | tf_op jit(solution)/shard_map/all_gather | solution.py:14
  159.2 7.8 while.62
  167.0 4.3 broadcast.28
  171.3 70.5 %while.64 = (s32[]{:T(128)}, f32[512,4096]{0,1:T(8,128)}, bf16[512,4096]{0,1:T(8,128)(2,1)}, bf16[512,4096]{0,1:T(8,128)(2,1)}, bf16[512,4096]{0,1:T(8,128)(2,1)...) while((s32[]{:T(128)}, f32[512,4096]{0,1:T(8,128)}, ...), condition=%wide.region_8.9_spmd.clone, body=%wide.region_7.8_spmd.clone.sunk | while | flops 543162368 | bytes 8964275 | solution.py:97
  175.4 3.6 fusion.66
  184.2 3.6 fusion.66
  193.0 3.6 fusion.66
  201.8 3.6 fusion.66
  210.6 3.6 fusion.66
  219.3 3.6 fusion.66
  228.2 3.6 fusion.66
  237.0 3.6 fusion.66
  243.8 69.3 %reduce-scatter.5.cloned.1.call-done = f32[512,512]{0,1:T(8,128)} async-done(((f32[512,4096]{0,1:T(8,128)}), f32[512,512]{0,1:T(8,128)}) %reduce-scatter.5.cloned.1.call-update) | async-done | bytes 1048592 | tf_op jit(solution)/shard_map/reduce_scatter | solution.py:100
  314.7 9.3 all_gather.27
  324.0 28.4 %all-gather.9.cloned.1.call-done = bf16[512,4096]{0,1:T(8,128)(2,1)} async-done(((bf16[512,512]{0,1:T(8,128)(2,1)}), bf16[512,4096]{0,1:T(8,128)(2,1)}) %all-gather.9.cloned.1.call-update) | async-done | bytes 4194320 | tf_op jit(solution)/shard_map/all_gather | solution.py:44
  352.4 4.3 broadcast.28.clone2.1
  356.6 4.3 broadcast.28.clone2
  360.9 4.2 broadcast.28.clone
  365.2 227.9 %while.65 = (s32[]{:T(128)}, f32[512,4096]{1,0:T(8,128)}, f32[512,4096]{1,0:T(8,128)}, f32[512,4096]{1,0:T(8,128)}, bf16[512,4096]{0,1:T(8,128)(2,1)}, /*index=5...) while((s32[]{:T(128)}, f32[512,4096]{1,0:T(8,128)}, ...), condition=%wide.region_12.13_spmd.clone, body=%wide.region_11.12_spmd.clone.sunk | while | flops 1358954496 | bytes 62769440 | solution.py:148
  372.5 2.1 fusion.79
  374.6 4.5 multiply_convert_fusion.2
  379.4 4.0 fusion.80
  383.4 4.5 fusion.78
  401.0 2.1 fusion.79
  403.1 4.5 multiply_convert_fusion.2
  407.9 4.0 fusion.80
  411.9 4.5 fusion.78
  429.6 2.1 fusion.79
  431.6 4.5 multiply_convert_fusion.2
  436.4 4.0 fusion.80
  440.4 4.5 fusion.78
  458.1 2.1 fusion.79
  460.2 4.5 multiply_convert_fusion.2
  465.0 4.0 fusion.80
  469.0 4.5 fusion.78
  486.6 2.1 fusion.79
  488.6 4.5 multiply_convert_fusion.2
  493.4 4.0 fusion.80
  497.4 4.5 fusion.78
  515.0 2.1 fusion.79
  517.1 4.5 multiply_convert_fusion.2
  521.9 4.0 fusion.80
  525.9 4.5 fusion.78
  543.5 2.1 fusion.79
  545.6 4.5 multiply_convert_fusion.2
  550.4 4.0 fusion.80
  554.4 4.5 fusion.78
  572.0 2.1 fusion.79
  574.0 4.5 multiply_convert_fusion.2
  578.8 4.0 fusion.80
  582.8 4.5 fusion.78
  595.7 68.9 %reduce-scatter.7.cloned.1.call-done = f32[512,512]{1,0:T(8,128)} async-done(((f32[512,4096]{1,0:T(8,128)}), f32[512,512]{1,0:T(8,128)}) %reduce-scatter.7.cloned.1.call-update) | async-done | bytes 1048592 | tf_op jit(solution)/shard_map/reduce_scatter | solution.py:149
  664.6 2.1 convert_element_type.38
  666.7 144.8 %reduce-scatter.11.cloned.1.call-done = f32[512,1024]{1,0:T(8,128)} async-done(((f32[512,4096]{1,0:T(8,128)}), f32[512,1024]{1,0:T(8,128)}) %reduce-scatter.11.cloned.1.call-update) | async-done | bytes 2097168 | tf_op jit(solution)/shard_map/reduce_scatter | solution.py:152
  811.4 2.7 convert_element_type.40
  814.2 144.9 %reduce-scatter.9.cloned.1.call-done = f32[512,1024]{1,0:T(8,128)} async-done(((f32[512,4096]{1,0:T(8,128)}), f32[512,1024]{1,0:T(8,128)}) %reduce-scatter.9.cloned.1.call-update) | async-done | bytes 2097168 | tf_op jit(solution)/shard_map/reduce_scatter | solution.py:151
  959.0 2.7 convert_element_type.39
  (262 shorter events, 216.4 us)
Async XLA Ops:
  7.2 8.8 copy-start.4
  7.2 8.8 copy-start.3
  7.2 42.7 %all-gather.7.cloned.1.call-start = ((), (), s32[]{:S(2)}) async-start(), calls=%async_computation.4 | async-start | bytes 4718592 | tf_op jit(solution)/shard_map/all_gather | solution.py:43
  9.3 123.0 %all-gather.11.cloned.1.call-start = ((), (), s32[]{:S(2)}) async-start(), calls=%async_computation.10 | async-start | bytes 1179648 | tf_op jit(solution)/shard_map/all_gather | solution.py:14
  107.9 0.7 copy-start.2
  108.6 49.6 %all-gather.13.cloned.1.call-start = ((), (), s32[]{:S(2)}) async-start(), calls=%async_computation.11 | async-start | bytes 1179648 | tf_op jit(solution)/shard_map/all_gather | solution.py:14
  109.4 203.8 %reduce-scatter.5.cloned.1.call-start = ((), (), s32[]{:S(2)}) async-start(), calls=%async_computation.5 | async-start | bytes 9437184 | tf_op jit(solution)/shard_map/reduce_scatter | solution.py:100
  241.7 1.0 copy-start.1
  241.8 110.6 %all-gather.9.cloned.1.call-start = ((), (), s32[]{:S(2)}) async-start(), calls=%async_computation.6 | async-start | bytes 4718592 | tf_op jit(solution)/shard_map/all_gather | solution.py:44
  243.8 420.8 %reduce-scatter.7.cloned.1.call-start = ((), (), s32[]{:S(2)}) async-start(), calls=%async_computation.7 | async-start | bytes 9437184 | tf_op jit(solution)/shard_map/reduce_scatter | solution.py:149
  593.1 218.3 %reduce-scatter.11.cloned.1.call-start = ((), (), s32[]{:S(2)}) async-start(), calls=%async_computation.9 | async-start | bytes 10485760 | tf_op jit(solution)/shard_map/reduce_scatter | solution.py:152
  593.2 1.5 copy-start
  593.9 365.2 %reduce-scatter.9.cloned.1.call-start = ((), (), s32[]{:S(2)}) async-start(), calls=%async_computation.8 | async-start | bytes 10485760 | tf_op jit(solution)/shard_map/reduce_scatter | solution.py:151
Sparse Core Ops, SparseCore 0:
  10.5 39.4 all-gather.6
  108.7 23.4 all-gather.10
  134.7 23.4 all-gather.12
  241.9 71.2 reduce-scatter.4
  315.6 36.7 all-gather.8
  593.2 71.3 reduce-scatter.6
  666.9 144.4 reduce-scatter.10
  813.8 145.1 reduce-scatter.8
where the time goes:
time: 973 us; the launch traced here: 969 us
  waiting for transfers between devices  534 us (55%)
  local copies, waits for them, and re-layouts  203 us (21%)
  matrix products  171 us (18%)
  other arithmetic  30.7 us (3%)
  between operations  14.2 us (1%)
    reduce_scatter x1, waiting for transfers between devices, body(): lax.psum_scatter(key_cells, 'dec', scatter_dimension=1, tiled=True)  145 us
    reduce_scatter x1, waiting for transfers between devices, body(): lax.psum_scatter(value_cells, 'dec', scatter_dimension=1, tiled=True)  145 us
    dynamic_slice x64, local copies, waits for them, and re-layouts, group_slice(): piece = lax.dynamic_slice_in_dim(source, column_start, group_width, 1)  70.9 us
    reduce_scatter x1, waiting for transfers between devices, body(): lax.psum_scatter(context_part, 'enc', scatter_dimension=1, tiled=True)  69.3 us
    reduce_scatter x1, waiting for transfers between devices, body(): lax.psum_scatter(query_part, 'enc', scatter_dimension=1, tiled=True)  68.9 us
    all_gather x2, waiting for transfers between devices, merged(): everything = jax.tree.map(lambda part: lax.all_gather(part, axis), shard)  41.3 us
    dot_general x8, matrix products, backward_group(): jnp.einsum('htc,chd->thd', score_grad, key_group, preferred_element_type=...  36.3 us
    dot_general x8, matrix products, backward_group(): jnp.einsum('thd,chd->htc', grad_group, value_group, preferred_element_typ...  35.6 us
  transfers between devices with their start and end apart: 8, of which 8 were waited for; matrix products, arithmetic and copies ran while one was open for 2% of the time, Pallas kernels for 0%

commit v1 on v0

v1 whole, which is shorter than its diff:
```python
import functools

import jax
import jax.numpy as jnp
import numpy as np
from jax import lax
from jax.experimental import pallas as pl
from jax.experimental.pallas import tpu as pltpu
from jax.sharding import PartitionSpec as P

DH = 64
BLOCK = 128
HIDDEN = -1e30
LANES = 128


def nt(a, b):
    return lax.dot_general(a, b, (((1,), (1,)), ((), ())), preferred_element_type=jnp.float32)


def nn(a, b):
    return lax.dot_general(a, b, (((1,), (0,)), ((), ())), preferred_element_type=jnp.float32)


def attention_kernel(
    heads, chunk, k_ref, v_ref, e_ref, q_ref, g_ref, bias_ref,
    ctx_ref, dq_ref, dk_ref, dv_ref,
    kt, vt, s_buf, e_buf, dk_acc, dv_acc,
):
    step = pl.program_id(0)
    cells, width = k_ref.shape
    rows = q_ref.shape[0]
    chunks = cells // chunk

    @pl.when(step == 0)
    def _():
        def prepare(i, _):
            at = pl.ds(pl.multiple_of(i * chunk, chunk), chunk)
            kt[:, at] = k_ref[at, :].T
            vt[:, at] = v_ref[at, :].T
            dk_acc[at, :] = jnp.zeros((chunk, width), jnp.float32)
            dv_acc[at, :] = jnp.zeros((chunk, width), jnp.float32)
            return 0

        lax.fori_loop(0, chunks, prepare, 0)

    lane = lax.broadcasted_iota(jnp.int32, (rows, width), 1)
    own = [(lane >= h * DH) & (lane < (h + 1) * DH) for h in range(heads)]
    q = q_ref[...]
    q_own = [jnp.where(own[h], q, jnp.zeros_like(q)) for h in range(heads)]
    q_aug = [jnp.concatenate([q_own[h], bias_ref[...]], axis=1) for h in range(heads)]

    def score_chunk(i, tops):
        at = pl.ds(pl.multiple_of(i * chunk, chunk), chunk)
        left = jnp.concatenate([k_ref[at, :], e_ref[at, :]], axis=1)
        out = []
        for h in range(heads):
            s = nt(left, q_aug[h])
            s_buf[h, at, :] = s
            out.append(jnp.maximum(tops[h], jnp.max(s.reshape(chunk // 8, 8, rows), axis=0)))
        return tuple(out)

    tops = lax.fori_loop(
        0, chunks, score_chunk, tuple(jnp.full((8, rows), -3e38, jnp.float32) for _ in range(heads))
    )
    top = [jnp.max(t, axis=0, keepdims=True) for t in tops]

    def weight_chunk(i, carry):
        at = pl.ds(pl.multiple_of(i * chunk, chunk), chunk)
        totals, outs = carry
        new_totals, new_outs = [], []
        for h in range(heads):
            e = jnp.exp(s_buf[h, at, :] - top[h])
            new_totals.append(totals[h] + jnp.sum(e.reshape(chunk // 8, 8, rows), axis=0))
            e = e.astype(jnp.bfloat16)
            e_buf[h, at, :] = e
            new_outs.append(outs[h] + nn(vt[h * DH : (h + 1) * DH, at], e))
        return tuple(new_totals), tuple(new_outs)

    totals, outs = lax.fori_loop(
        0,
        chunks,
        weight_chunk,
        (
            tuple(jnp.zeros((8, rows), jnp.float32) for _ in range(heads)),
            tuple(jnp.zeros((DH, rows), jnp.float32) for _ in range(heads)),
        ),
    )
    inv = [1.0 / jnp.sum(t, axis=0, keepdims=True) for t in totals]
    stack = jnp.concatenate(
        [outs[h] * inv[h] for h in range(heads)]
        + [jnp.broadcast_to(inv[h], (DH, rows)) for h in range(heads)],
        axis=0,
    ).T
    attended = stack[:, :width]
    ctx_ref[...] = attended.astype(ctx_ref.dtype)
    g_scaled = (g_ref[...].astype(jnp.float32) * stack[:, width:]).astype(jnp.bfloat16)
    product = g_scaled.astype(jnp.float32) * attended
    lane_aug = lax.broadcasted_iota(jnp.int32, (rows, LANES), 1)
    g_own, g_aug = [], []
    for h in range(heads):
        term = -jnp.sum(jnp.where(own[h], product, 0.0), axis=1, keepdims=True)
        high = term.astype(jnp.bfloat16).astype(jnp.float32)
        low = term - high
        extra = jnp.where(
            lane_aug == LANES - 1, high, jnp.where(lane_aug == LANES - 2, low, 0.0)
        ).astype(jnp.bfloat16)
        g_own.append(jnp.where(own[h], g_scaled, jnp.zeros_like(g_scaled)))
        g_aug.append(jnp.concatenate([g_own[h], extra], axis=1))
    q_all = jnp.concatenate(q_own, axis=0)
    g_all = jnp.concatenate(g_own, axis=0)

    def grad_chunk(i, dqs):
        at = pl.ds(pl.multiple_of(i * chunk, chunk), chunk)
        left = jnp.concatenate([v_ref[at, :], e_ref[at, :]], axis=1)
        new_dqs, ds_all, e_all = [], [], []
        for h in range(heads):
            e = e_buf[h, at, :]
            ds = (e.astype(jnp.float32) * nt(left, g_aug[h])).astype(jnp.bfloat16)
            new_dqs.append(dqs[h] + nn(kt[h * DH : (h + 1) * DH, at], ds))
            ds_all.append(ds)
            e_all.append(e)
        dk_acc[at, :] += nn(jnp.concatenate(ds_all, axis=1), q_all)
        dv_acc[at, :] += nn(jnp.concatenate(e_all, axis=1), g_all)
        return tuple(new_dqs)

    dqs = lax.fori_loop(
        0, chunks, grad_chunk, tuple(jnp.zeros((DH, rows), jnp.float32) for _ in range(heads))
    )
    dq_ref[...] = jnp.concatenate(dqs, axis=0).T.astype(dq_ref.dtype)

    @pl.when(step == pl.num_programs(0) - 1)
    def _():
        dk_ref[...] = dk_acc[...].astype(dk_ref.dtype)
        dv_ref[...] = dv_acc[...].astype(dv_ref.dtype)


def cell_marks(cells):
    block_ids = lax.broadcasted_iota(jnp.int32, (cells, LANES), 0) // BLOCK
    lane = lax.broadcasted_iota(jnp.int32, (cells, LANES), 1)
    return ((block_ids == lane) | (lane >= LANES - 2)).astype(jnp.bfloat16)


def attention(q, g, k, v, bias, grad_type=jnp.bfloat16, rows=256, chunk=512):
    tokens, width = q.shape
    cells = k.shape[0]
    heads = width // DH
    whole = lambda i: (0, 0)
    part = lambda i: (i, 0)
    cell_spec = pl.BlockSpec((cells, width), whole)
    token_spec = pl.BlockSpec((rows, width), part)
    bf = jnp.bfloat16
    return pl.pallas_call(
        functools.partial(attention_kernel, heads, chunk),
        grid=(tokens // rows,),
        out_shape=(
            jax.ShapeDtypeStruct((tokens, width), bf),
            jax.ShapeDtypeStruct((tokens, width), bf),
            jax.ShapeDtypeStruct((cells, width), grad_type),
            jax.ShapeDtypeStruct((cells, width), grad_type),
        ),
        in_specs=[
            cell_spec,
            cell_spec,
            pl.BlockSpec((cells, LANES), whole),
            token_spec,
            token_spec,
            pl.BlockSpec((rows, LANES), part),
        ],
        out_specs=(token_spec, token_spec, cell_spec, cell_spec),
        scratch_shapes=[
            pltpu.VMEM((width, cells), bf),
            pltpu.VMEM((width, cells), bf),
            pltpu.VMEM((heads, cells, rows), jnp.float32),
            pltpu.VMEM((heads, cells, rows), bf),
            pltpu.VMEM((cells, width), jnp.float32),
            pltpu.VMEM((cells, width), jnp.float32),
        ],
        compiler_params=pltpu.CompilerParams(vmem_limit_bytes=60 * 1024 * 1024),
        name="attention",
    )(k, v, cell_marks(cells), q, g, bias)


def hidden_blocks(ref_blocks, ref_counts):
    slot_ids = jnp.arange(ref_blocks.shape[1], dtype=jnp.int32)
    live = slot_ids[None, :] < ref_counts[:, None]
    lane = jnp.arange(LANES, dtype=jnp.int32)
    seen = jnp.any((ref_blocks[:, :, None] == lane) & live[:, :, None], axis=1)
    return jnp.where(seen | (lane >= LANES - 2), 0.0, HIDDEN).astype(jnp.bfloat16)


def shared_head(q, g, k, v, bias, per, dec):
    share = DH // q.shape[1]
    mates = [
        [per * (j + i) + c for i in range(share)] for c in range(per) for j in range(0, dec, share)
    ]
    place = lax.rem(lax.axis_index("enc") // per, share)
    rows = q.shape[0] // share

    def to_head(x):
        return lax.all_to_all(x, "enc", 0, 1, axis_index_groups=mates, tiled=True)

    def from_head(x):
        return lax.all_to_all(x, "enc", 1, 0, axis_index_groups=mates, tiled=True)

    def widen(x):
        return lax.all_gather(x, "enc", axis=1, axis_index_groups=mates, tiled=True)

    def add_up(x):
        total = lax.psum_scatter(
            x, "enc", scatter_dimension=1, axis_index_groups=mates, tiled=True
        )
        return total.astype(jnp.bfloat16)

    bias = lax.dynamic_slice_in_dim(bias, place * rows, rows, 0)
    ctx, dq, dk, dv = attention(to_head(q), to_head(g), widen(k), widen(v), bias, jnp.float32)
    return from_head(ctx), from_head(dq), add_up(dk), add_up(dv)


def body(queries, out_grad, memory_keys, memory_values, ref_blocks, ref_counts):
    enc, dec = lax.axis_size("enc"), lax.axis_size("dec")
    per = enc // dec
    tok, tok_width = queries.shape
    own_cells, full = memory_keys.shape
    width = full // (enc * dec)
    groups = [[per * k + c for k in range(dec)] for c in range(per)]

    def token_in(x):
        x = x.reshape(tok, dec, width).transpose(1, 0, 2)
        x = lax.all_to_all(x, "enc", 0, 0, axis_index_groups=groups)
        return lax.all_to_all(x, "dec", 0, 0).reshape(dec * tok, width)

    def token_out(x):
        x = lax.all_to_all(x.reshape(dec, tok, width), "dec", 0, 0)
        x = lax.all_to_all(x, "enc", 0, 0, axis_index_groups=groups)
        return x.transpose(1, 0, 2).reshape(tok, tok_width)

    def cell_in(x):
        x = lax.dynamic_slice_in_dim(x, lax.axis_index("dec") * (full // dec), full // dec, 1)
        x = x.reshape(own_cells, per, dec, width).transpose(2, 1, 0, 3)
        x = lax.all_to_all(x.reshape(enc, own_cells, width), "enc", 0, 0)
        return x.reshape(enc * own_cells, width)

    def cell_out(x):
        x = lax.all_to_all(x.reshape(enc, own_cells, width), "enc", 0, 0)
        x = x.reshape(dec, per, own_cells, width).transpose(2, 1, 0, 3)
        return x.reshape(own_cells, full // dec)

    bias = lax.all_gather(hidden_blocks(ref_blocks, ref_counts), "dec", tiled=True)
    q, g, k, v = token_in(queries), token_in(out_grad), cell_in(memory_keys), cell_in(memory_values)
    if width >= DH:
        ctx, dq, dk, dv = attention(q, g, k, v, bias)
    else:
        ctx, dq, dk, dv = shared_head(q, g, k, v, bias, per, dec)
    return token_out(ctx), token_out(dq), cell_out(dk), cell_out(dv)


def solution(mesh):
    in_specs = (
        P("dec", "enc"),
        P("dec", "enc"),
        P("enc", None),
        P("enc", None),
        P("dec", None),
        P("dec"),
    )
    out_specs = (P("dec", "enc"), P("dec", "enc"), P("enc", "dec"), P("enc", "dec"))
    return jax.shard_map(body, mesh=mesh, in_specs=in_specs, out_specs=out_specs, check_vma=False)
```

time: 973 us -> 319 us (0.33)
  waiting for transfers between devices: 534 us -> 44.6 us
  local copies, waits for them, and re-layouts: 203 us -> 19.3 us
  matrix products: 171 us -> 0 us
  Pallas kernels: 0 us -> 119 us
  blocking collectives: 9.27 us -> 97.8 us
  starting transfers between devices: 0.32 us -> 29 us
  other arithmetic: 30.7 us -> 7.78 us
  between operations: 14.2 us -> 0.81 us
    reduce_scatter x4 -> x0, waiting for transfers between devices: 428 us -> none  [the longest x1 145 us: body(): lax.psum_scatter(key_cells, 'dec', scatter_dimension=1, tiled=True)]
    dot_general x56 -> x0, matrix products: 171 us -> none  [the longest x8 36.3 us: backward_group(): jnp.einsum('htc,chd->thd', score_grad, key_group, preferred_element_type=...]
    pallas_call x0 -> x1, Pallas kernels: none -> 119 us  [attention(): pl.pallas_call(functools.partial(attention_kernel, heads, chunk), grid=(t...]
    all_gather x4 -> x0, waiting for transfers between devices: 104 us -> none  [the longest x2 41.3 us: merged(): everything = jax.tree.map(lambda part: lax.all_gather(part, axis), shard)]
    all_to_all x0 -> x5, blocking collectives: none -> 77.6 us  [the longest x2 38 us: cell_out(): x = lax.all_to_all(x.reshape(enc, own_cells, width), 'enc', 0, 0)]
    dynamic_slice x72 -> x1, local copies, waits for them, and re-layouts: 75.5 us -> 1.72 us  [cell_in(): lax.dynamic_slice_in_dim(x, lax.axis_index('dec') * (full // dec), full /...]
    dynamic_update_slice x56 -> x0, local copies, waits for them, and re-layouts: 61.7 us -> none  [the longest x16 21.1 us: backward_group(): lax.dynamic_update_slice_in_dim(query_acc, query_term.reshape(token_count...]
    all_to_all x0 -> x7, waiting for transfers between devices: none -> 44.6 us  [the longest x2 28.7 us: cell_in(): x = lax.all_to_all(x.reshape(enc, own_cells, width), 'enc', 0, 0)]
  transfers between devices with their start and end apart: 8 -> 7, of which waited for: 8 -> 5; matrix products, arithmetic and copies ran while one was open for 2% -> 7% of each run, Pallas kernels for 0% -> 0%
where the time goes in v1:
time: 319 us; the launch traced here: 318 us
  Pallas kernels  119 us (37%)
  blocking collectives  97.8 us (31%)
  waiting for transfers between devices  44.6 us (14%)
  starting transfers between devices  29 us (9%)
  local copies, waits for them, and re-layouts  19.3 us (6%)
  other arithmetic  7.78 us (2%)
    pallas_call x1, Pallas kernels, attention(): pl.pallas_call(functools.partial(attention_kernel, heads, chunk), grid=(t...  119 us
    all_to_all x2, blocking collectives, cell_out(): x = lax.all_to_all(x.reshape(enc, own_cells, width), 'enc', 0, 0)  38 us
    all_to_all x2, waiting for transfers between devices, cell_in(): x = lax.all_to_all(x.reshape(enc, own_cells, width), 'enc', 0, 0)  28.7 us
    all_to_all x2, blocking collectives, token_out(): x = lax.all_to_all(x.reshape(dec, tok, width), 'dec', 0, 0)  28.4 us
    all_gather x1, blocking collectives, body(): lax.all_gather(hidden_blocks(ref_blocks, ref_counts), 'dec', tiled=True)  20.2 us
    all_to_all x1, blocking collectives, token_out(): x = lax.all_to_all(x, 'enc', 0, 0, axis_index_groups=groups)  11.2 us
    all_to_all x2, waiting for transfers between devices, token_in(): x = lax.all_to_all(x, 'enc', 0, 0, axis_index_groups=groups)  10.1 us
    all_to_all x2, starting transfers between devices, token_in(): x = lax.all_to_all(x, 'enc', 0, 0, axis_index_groups=groups)  9.31 us
  transfers between devices with their start and end apart: 7, of which 5 were waited for; matrix products, arithmetic and copies ran while one was open for 7% of the time, Pallas kernels for 0%

profile of v1, /device:TPU:0, one launch (start us, length us, event | category | flops | bytes accessed | tf_op | source)
XLA Modules:
  0.0 318.2 jit_solution(6423975934917673788)
XLA Ops:
  0.6 0.0 copy-start
  0.6 0.0 copy-start.7
  0.7 1.0 copy-done
  1.7 0.9 bitcast_bitcast_fusion.1
  2.6 5.2 %all-to-all-start.2 = ((bf16[4,512,128]{2,1,0:T(8,128)(2,1)}), bf16[4,512,128]{2,1,0:T(8,128)(2,1)}, u32[]{:S(2)}, u32[]{:S(2)}) async-start(bf16[4,512,128]{2,1,0:T(8,128)(2,1)} %bitcast_bitcast_fusion.1), calls=%async_computation.2 | async-start | bytes 1048576 | tf_op jit(solution)/shard_map/all_to_all | solution.py:230
  7.7 0.0 copy-done.7
  7.7 0.9 bitcast_bitcast_fusion
  8.6 7.7 %all-to-all-done.2 = bf16[4,512,128]{2,1,0:T(8,128)(2,1)} async-done(((bf16[4,512,128]{2,1,0:T(8,128)(2,1)}), bf16[4,512,128]{2,1,0:T(8,128)(2,1)}, u32[]{:S(2)}, u32[]{:S(2)}) %all-to-all-start.2) | async-done | bytes 524320 | tf_op jit(solution)/shard_map/all_to_all | solution.py:230
  16.3 4.1 %all-to-all-start.4 = ((bf16[4,512,128]{2,1,0:T(8,128)(2,1)}), bf16[4,512,128]{2,1,0:T(8,128)(2,1)}, u32[]{:S(2)}, u32[]{:S(2)}) async-start(bf16[4,512,128]{2,1,0:T(8,128)(2,1)} %bitcast_bitcast_fusion), calls=%async_computation.4 | async-start | bytes 1048576 | tf_op jit(solution)/shard_map/all_to_all | solution.py:230
  20.4 1.7 constant_dynamic-slice_fusion
  22.2 1.3 copy.49
  23.5 2.3 copy.40
  25.8 2.4 all-to-all-done.4
  28.2 4.2 %all-to-all-start.1 = ((bf16[8,512,128]{2,1,0:T(8,128)(2,1)}), bf16[8,512,128]{2,1,0:T(8,128)(2,1)}, u32[]{:S(2)}, u32[]{:S(2)}) async-start(bf16[8,512,128]{2,1,0:T(8,128)(2,1)} %bitcast.6), calls=%async_computation.1 | async-start | bytes 2097152 | tf_op jit(solution)/shard_map/all_to_all | solution.py:241
  32.4 0.5 copy.48
  33.0 0.0 copy-start.9
  33.0 1.3 copy.38
  34.3 0.0 copy-start.8
  34.3 13.5 %all-to-all-done.1 = bf16[8,512,128]{2,1,0:T(8,128)(2,1)} async-done(((bf16[8,512,128]{2,1,0:T(8,128)(2,1)}), bf16[8,512,128]{2,1,0:T(8,128)(2,1)}, u32[]{:S(2)}, u32[]{:S(2)}) %all-to-all-start.1) | async-done | bytes 1048608 | tf_op jit(solution)/shard_map/all_to_all | solution.py:241
  47.8 3.6 %all-to-all-start = ((bf16[8,512,128]{2,1,0:T(8,128)(2,1)}), bf16[8,512,128]{2,1,0:T(8,128)(2,1)S(1)}, u32[]{:S(2)}, u32[]{:S(2)}) async-start(bf16[8,512,128]{2,1,0:T(8,128)(2,1)} %bitcast.2), calls=%async_computation | async-start | bytes 2097152 | tf_op jit(solution)/shard_map/all_to_all | solution.py:241
  51.4 0.0 copy-done.9
  51.4 0.1 iota_compare_fusion.2
  51.6 15.2 %all-to-all-done = bf16[8,512,128]{2,1,0:T(8,128)(2,1)S(1)} async-done(((bf16[8,512,128]{2,1,0:T(8,128)(2,1)}), bf16[8,512,128]{2,1,0:T(8,128)(2,1)S(1)}, u32[]{:S(2)}, u32[]{:S(2)}) %all-to-all-start) | async-done | bytes 1048608 | tf_op jit(solution)/shard_map/all_to_all | solution.py:241
  66.7 0.0 copy-start.1
  66.7 4.9 %all-to-all-start.3 = ((bf16[4,512,128]{2,1,0:T(8,128)(2,1)}), bf16[4,512,128]{2,1,0:T(8,128)(2,1)S(1)}, u32[]{:S(2)}, u32[]{:S(2)}) async-start(bf16[4,512,128]{2,1,0:T(8,128)(2,1)} %all-to-all-done.2), calls=%async_computation.3 | async-start | bytes 1048576 | tf_op jit(solution)/shard_map/all_to_all | solution.py:231
  71.7 0.0 copy-done.8
  71.7 0.1 copy.43
  71.8 2.9 fusion.3
  74.7 20.2 %all_gather.3.bias_ref = bf16[2048,128]{1,0:T(8,128)(2,1)} all-gather(bf16[512,128]{1,0:T(8,128)(2,1)S(1)} %select_convert_fusion), channel_id=1, replica_groups=mesh['enc'=8,'dec'=4] {'dec'}, dimensions={0}, use_global_device_ids=true | all-gather | bytes 655360 | tf_op jit(solution)/shard_map/all_gather | solution.py:249
  94.9 0.0 all-to-all-done.3
  94.9 0.0 copy-start.2
  94.9 3.5 %all-to-all-start.5 = ((bf16[4,512,128]{2,1,0:T(8,128)(2,1)}), bf16[4,512,128]{2,1,0:T(8,128)(2,1)S(1)}, u32[]{:S(2)}, u32[]{:S(2)}) async-start(bf16[4,512,128]{2,1,0:T(8,128)(2,1)} %all-to-all-done.4), calls=%async_computation.5 | async-start | bytes 1048576 | tf_op jit(solution)/shard_map/all_to_all | solution.py:231
  98.4 4.7 %fusion.1.e_ref = bf16[4096,128]{1,0:T(8,128)(2,1)} fusion(s32[4096]{0:T(1024)S(1)} %get-tuple-element.14, s32[4096]{0:T(1024)S(1)} %get-tuple-element.15, pred[4096]{0:T(1024)(128)(4,1)S(1)} %fusion.6, pred[128]{0:T(512)(128)(4,1)S(1)} %iota_compare_fusion.3), kind=kLoop, calls=%fused_computation.3 | loop fusion | flops 2097152 | bytes 1085568 | tf_op jit(solution)/shard_map/convert_element_type | solution.py:141
  103.1 0.0 copy-done.1
  103.1 5.8 %all-to-all-done.5 = bf16[4,512,128]{2,1,0:T(8,128)(2,1)S(1)} async-done(((bf16[4,512,128]{2,1,0:T(8,128)(2,1)}), bf16[4,512,128]{2,1,0:T(8,128)(2,1)S(1)}, u32[]{:S(2)}, u32[]{:S(2)}) %all-to-all-start.5) | async-done | bytes 524320 | tf_op jit(solution)/shard_map/all_to_all | solution.py:231
  108.9 0.0 copy-start.3
  108.9 0.0 copy-done.2
  108.9 0.8 copy-done.3
  109.7 118.9 %attention.1 = (bf16[2048,128]{1,0:T(8,128)(2,1)}, bf16[2048,128]{1,0:T(8,128)(2,1)}, bf16[4096,128]{1,0:T(8,128)(2,1)}, bf16[4096,128]{1,0:T(8,128)(2,1)}) custom-call(bf16[4096,128]{1,0:T(8,128)(2,1)} %bitcast.56, bf16[4096,128]{1,0:T(8,128)(2,1)} %bitcast.7.v_ref, bf16[4096,128]{1,0:T(8,128)(2,1)} %fusion.1.e_ref, bf16[2048,128]{1,0:T(8,128)(2,1)} %bitcast.57, ...), custom_call_target="tpu_custom_call" | custom-call | tf_op jit(solution)/shard_map/attention/pallas_call | solution.py:153
  228.6 0.0 copy-start.6
  228.6 0.0 copy-start.5
  228.6 13.9 %all_to_all.60 = bf16[4,512,128]{2,1,0:T(8,128)(2,1)S(1)} all-to-all(bf16[4,512,128]{2,1,0:T(8,128)(2,1)} %bitcast.62), channel_id=1, replica_groups=mesh['enc'=8,'dec'=4] {'dec'}, dimensions={0} | all-to-all | bytes 1048576 | tf_op jit(solution)/shard_map/all_to_all | solution.py:234
  242.5 14.5 %all_to_all.61 = bf16[4,512,128]{2,1,0:T(8,128)(2,1)} all-to-all(bf16[4,512,128]{2,1,0:T(8,128)(2,1)} %bitcast.61), channel_id=1, replica_groups=mesh['enc'=8,'dec'=4] {'dec'}, dimensions={0} | all-to-all | bytes 1048576 | tf_op jit(solution)/shard_map/all_to_all | solution.py:234
  257.0 0.0 copy-done.6
  257.0 20.3 %all_to_all.62 = bf16[8,512,128]{2,1,0:T(8,128)(2,1)S(1)} all-to-all(bf16[8,512,128]{2,1,0:T(8,128)(2,1)S(1)} %bitcast.60), channel_id=1, replica_groups=mesh['enc'=8,'dec'=4] {'enc'}, dimensions={0} | all-to-all | bytes 2097152 | tf_op jit(solution)/shard_map/all_to_all | solution.py:245
  277.3 0.0 copy-done.5
  277.3 17.8 %all_to_all.63 = bf16[8,512,128]{2,1,0:T(8,128)(2,1)S(1)} all-to-all(bf16[8,512,128]{2,1,0:T(8,128)(2,1)S(1)} %bitcast.59), channel_id=1, replica_groups=mesh['enc'=8,'dec'=4] {'enc'}, dimensions={0} | all-to-all | bytes 2097152 | tf_op jit(solution)/shard_map/all_to_all | solution.py:245
  295.0 11.2 %all_to_all.64 = bf16[4,512,128]{2,1,0:T(8,128)(2,1)} all-to-all(bf16[4,512,128]{2,1,0:T(8,128)(2,1)S(1)} %all_to_all.60), channel_id=1, replica_groups={{0,8,16,24},{4,12,20,28},{1,9,17,25},{5,13,21,29},{2,10,18,26},{6,14,22..., dimensions={0} | all-to-all | bytes 1048576 | tf_op jit(solution)/shard_map/all_to_all | solution.py:235
  306.2 3.5 %all-to-all-start.7 = ((bf16[4,512,128]{2,1,0:T(8,128)(2,1)}), bf16[4,512,128]{2,1,0:T(8,128)(2,1)S(1)}, u32[]{:S(2)}, u32[]{:S(2)}) async-start(bf16[4,512,128]{2,1,0:T(8,128)(2,1)} %all_to_all.61), calls=%async_computation.7 | async-start | bytes 1048576 | tf_op jit(solution)/shard_map/all_to_all | solution.py:235
  309.7 1.8 copy.61
  311.5 2.6 reshape.110
  314.1 0.8 copy.60
  314.9 0.0 copy-start.4
  314.9 1.5 reshape.113
  316.4 0.0 copy-done.4
  316.5 0.9 copy_bitcast_fusion.2
  317.3 0.0 all-to-all-done.7
  317.3 0.9 copy_bitcast_fusion.3
  (4 shorter events, 0.1 us)
Async XLA Ops:
  0.6 1.0 copy-start
  0.6 7.1 %copy-start.7 = (bf16[512,512]{1,0:T(8,128)(2,1)S(1)}, bf16[512,512]{1,0:T(8,128)(2,1)}, u32[]{:S(2)}) copy-start(bf16[512,512]{1,0:T(8,128)(2,1)} %param.7) | copy-start | bytes 1572868
  2.6 13.7 %all-to-all-start.2 = ((bf16[4,512,128]{2,1,0:T(8,128)(2,1)}), bf16[4,512,128]{2,1,0:T(8,128)(2,1)}, u32[]{:S(2)}, u32[]{:S(2)}) async-start(bf16[4,512,128]{2,1,0:T(8,128)(2,1)} %bitcast_bitcast_fusion.1), calls=%async_computation.2 | async-start | bytes 1048576 | tf_op jit(solution)/shard_map/all_to_all | solution.py:230
  16.3 11.9 %all-to-all-start.4 = ((bf16[4,512,128]{2,1,0:T(8,128)(2,1)}), bf16[4,512,128]{2,1,0:T(8,128)(2,1)}, u32[]{:S(2)}, u32[]{:S(2)}) async-start(bf16[4,512,128]{2,1,0:T(8,128)(2,1)} %bitcast_bitcast_fusion), calls=%async_computation.4 | async-start | bytes 1048576 | tf_op jit(solution)/shard_map/all_to_all | solution.py:230
  28.2 19.7 %all-to-all-start.1 = ((bf16[8,512,128]{2,1,0:T(8,128)(2,1)}), bf16[8,512,128]{2,1,0:T(8,128)(2,1)}, u32[]{:S(2)}, u32[]{:S(2)}) async-start(bf16[8,512,128]{2,1,0:T(8,128)(2,1)} %bitcast.6), calls=%async_computation.1 | async-start | bytes 2097152 | tf_op jit(solution)/shard_map/all_to_all | solution.py:241
  33.0 18.5 %copy-start.9 = (s32[512]{0:T(512)S(1)}, s32[512]{0:T(512)}, u32[]{:S(2)}) copy-start(s32[512]{0:T(512)} %param.11) | copy-start | bytes 6148
  34.3 37.4 %copy-start.8 = (s32[512,8]{0,1:T(8,128)S(1)}, s32[512,8]{0,1:T(8,128)}, u32[]{:S(2)}) copy-start(s32[512,8]{0,1:T(8,128)} %param.10) | copy-start | bytes 49156
  47.8 18.9 %all-to-all-start = ((bf16[8,512,128]{2,1,0:T(8,128)(2,1)}), bf16[8,512,128]{2,1,0:T(8,128)(2,1)S(1)}, u32[]{:S(2)}, u32[]{:S(2)}) async-start(bf16[8,512,128]{2,1,0:T(8,128)(2,1)} %bitcast.2), calls=%async_computation | async-start | bytes 2097152 | tf_op jit(solution)/shard_map/all_to_all | solution.py:241
  66.7 36.4 %copy-start.1 = (bf16[8,512,128]{2,1,0:T(8,128)(2,1)}, bf16[8,512,128]{2,1,0:T(8,128)(2,1)S(1)}, u32[]{:S(2)}) copy-start(bf16[8,512,128]{2,1,0:T(8,128)(2,1)S(1)} %all-to-all-done) | copy-start | bytes 3145732
  66.7 28.2 %all-to-all-start.3 = ((bf16[4,512,128]{2,1,0:T(8,128)(2,1)}), bf16[4,512,128]{2,1,0:T(8,128)(2,1)S(1)}, u32[]{:S(2)}, u32[]{:S(2)}) async-start(bf16[4,512,128]{2,1,0:T(8,128)(2,1)} %all-to-all-done.2), calls=%async_computation.3 | async-start | bytes 1048576 | tf_op jit(solution)/shard_map/all_to_all | solution.py:231
  94.9 14.0 %copy-start.2 = (bf16[4,512,128]{2,1,0:T(8,128)(2,1)}, bf16[4,512,128]{2,1,0:T(8,128)(2,1)S(1)}, u32[]{:S(2)}) copy-start(bf16[4,512,128]{2,1,0:T(8,128)(2,1)S(1)} %all-to-all-done.3) | copy-start | bytes 1572868
  94.9 14.0 %all-to-all-start.5 = ((bf16[4,512,128]{2,1,0:T(8,128)(2,1)}), bf16[4,512,128]{2,1,0:T(8,128)(2,1)S(1)}, u32[]{:S(2)}, u32[]{:S(2)}) async-start(bf16[4,512,128]{2,1,0:T(8,128)(2,1)} %all-to-all-done.4), calls=%async_computation.5 | async-start | bytes 1048576 | tf_op jit(solution)/shard_map/all_to_all | solution.py:231
  108.9 0.8 copy-start.3
  228.6 28.4 %copy-start.6 = (bf16[4096,128]{1,0:T(8,128)(2,1)S(1)}, bf16[4096,128]{1,0:T(8,128)(2,1)}, u32[]{:S(2)}) copy-start(bf16[4096,128]{1,0:T(8,128)(2,1)} %get-tuple-element.10) | copy-start | bytes 3145732
  228.6 48.6 %copy-start.5 = (bf16[4096,128]{1,0:T(8,128)(2,1)S(1)}, bf16[4096,128]{1,0:T(8,128)(2,1)}, u32[]{:S(2)}) copy-start(bf16[4096,128]{1,0:T(8,128)(2,1)} %get-tuple-element.11) | copy-start | bytes 3145732
  306.2 11.1 %all-to-all-start.7 = ((bf16[4,512,128]{2,1,0:T(8,128)(2,1)}), bf16[4,512,128]{2,1,0:T(8,128)(2,1)S(1)}, u32[]{:S(2)}, u32[]{:S(2)}) async-start(bf16[4,512,128]{2,1,0:T(8,128)(2,1)} %all_to_all.61), calls=%async_computation.7 | async-start | bytes 1048576 | tf_op jit(solution)/shard_map/all_to_all | solution.py:235
  314.9 1.6 copy-start.4

commit v2 on v1

--- a/solution.py
+++ b/solution.py
@@ -48,7 +48,10 @@
     own = [(lane >= h * DH) & (lane < (h + 1) * DH) for h in range(heads)]
     q = q_ref[...]
     q_own = [jnp.where(own[h], q, jnp.zeros_like(q)) for h in range(heads)]
-    q_aug = [jnp.concatenate([q_own[h], bias_ref[...]], axis=1) for h in range(heads)]
+    bias = bias_ref[...].astype(jnp.float32)
+    blank = jnp.zeros((LANES - bias.shape[0], rows), jnp.float32)
+    bias = jnp.concatenate([bias, blank], axis=0).T.astype(jnp.bfloat16)
+    q_aug = [jnp.concatenate([q_own[h], bias], axis=1) for h in range(heads)]
 
     def score_chunk(i, tops):
         at = pl.ds(pl.multiple_of(i * chunk, chunk), chunk)
@@ -165,7 +168,7 @@
             pl.BlockSpec((cells, LANES), whole),
             token_spec,
             token_spec,
-            pl.BlockSpec((rows, LANES), part),
+            pl.BlockSpec((bias.shape[0], rows), lambda i: (0, i)),
         ],
         out_specs=(token_spec, token_spec, cell_spec, cell_spec),
         scratch_shapes=[
@@ -181,12 +184,244 @@
     )(k, v, cell_marks(cells), q, g, bias)
 
 
-def hidden_blocks(ref_blocks, ref_counts):
+def hidden_blocks(ref_blocks, ref_counts, blocks):
     slot_ids = jnp.arange(ref_blocks.shape[1], dtype=jnp.int32)
     live = slot_ids[None, :] < ref_counts[:, None]
-    lane = jnp.arange(LANES, dtype=jnp.int32)
-    seen = jnp.any((ref_blocks[:, :, None] == lane) & live[:, :, None], axis=1)
-    return jnp.where(seen | (lane >= LANES - 2), 0.0, HIDDEN).astype(jnp.bfloat16)
+    wanted = jnp.where(live, ref_blocks, -1).T
+    seen = jnp.any(wanted[:, None, :] == jnp.arange(blocks, dtype=jnp.int32)[:, None], axis=0)
+    return jnp.where(seen, 0.0, HIDDEN).astype(jnp.bfloat16)
+
+
+def greet_all():
+    barrier = pltpu.get_barrier_semaphore()
+    enc, dec = lax.axis_size("enc"), lax.axis_size("dec")
+    me = lax.axis_index("enc") * dec + lax.axis_index("dec")
+
+    def greet(d, _):
+        other = lax.rem(me + d, enc * dec)
+        pl.semaphore_signal(
+            barrier, inc=1, device_id=(other // dec, lax.rem(other, dec)),
+            device_id_type=pl.DeviceIdType.MESH,
+        )
+        return 0
+
+    lax.fori_loop(1, enc * dec, greet, 0)
+    pl.semaphore_wait(barrier, enc * dec - 1)
+
+
+def remote(src, dst, send, recv, target):
+    return pltpu.make_async_remote_copy(
+        src_ref=src, dst_ref=dst, send_sem=send, recv_sem=recv,
+        device_id=target, device_id_type=pl.DeviceIdType.MESH,
+    )
+
+
+def lanes(ref, index, width):
+    return ref.at[:, pl.ds(pl.multiple_of(index * width, width), width)]
+
+
+def rows_of(ref, index, count):
+    return ref.at[pl.ds(pl.multiple_of(index * count, count), count), :]
+
+
+def scatter_kernel(
+    q, k, bias, g, v, q_all, k_all, bias_all, g_all, v_all,
+    tok_send, tok_recv, cell_send, cell_recv, bias_send, bias_recv, local,
+):
+    enc, dec = lax.axis_size("enc"), lax.axis_size("dec")
+    per = enc // dec
+    e, z = lax.axis_index("enc"), lax.axis_index("dec")
+    width = k_all.shape[1]
+    tok, cells = q.shape[0], k.shape[0]
+    home, core = e // per, lax.rem(e, per)
+    slot = lambda x: z * enc + lax.rem(x, per) * dec + x // per
+    greet_all()
+
+    def token_copy(n, src, dst, i):
+        return remote(
+            lanes(src, i, width), rows_of(dst, z, tok),
+            tok_send.at[n, i], tok_recv.at[n, z], (per * i + core, home),
+        )
+
+    def token_wait(n, src, dst, i):
+        return remote(
+            lanes(src, 0, width), rows_of(dst, i, tok),
+            tok_send.at[n, 0], tok_recv.at[n, i], (e, z),
+        )
+
+    def token_own(n, src, dst):
+        return pltpu.make_async_copy(lanes(src, home, width), rows_of(dst, z, tok), local.at[n])
+
+    def cell_copy(n, src, dst, j):
+        target = lax.rem(e + j, enc)
+        return remote(
+            lanes(src, slot(target), width), rows_of(dst, e, cells),
+            cell_send.at[n, j - 1], cell_recv.at[n, j - 1], (target, z),
+        )
+
+    def cell_wait(n, src, dst, j):
+        origin = lax.rem(e - j + enc, enc)
+        return remote(
+            lanes(src, 0, width), rows_of(dst, origin, cells),
+            cell_send.at[n, j - 1], cell_recv.at[n, j - 1], (origin, z),
+        )
+
+    def cell_own(n, src, dst):
+        return pltpu.make_async_copy(
+            lanes(src, slot(e), width), rows_of(dst, e, cells), local.at[2 + n]
+        )
+
+    def bias_copy(j):
+        target = lax.rem(z + j, dec)
+        return remote(
+            bias, lanes(bias_all, z, tok), bias_send.at[j - 1], bias_recv.at[j - 1], (e, target)
+        )
+
+    def bias_wait(j):
+        origin = lax.rem(z - j + dec, dec)
+        return remote(
+            bias, lanes(bias_all, origin, tok), bias_send.at[j - 1], bias_recv.at[j - 1], (e, origin)
+        )
+
+    bias_own = pltpu.make_async_copy(bias, lanes(bias_all, z, tok), local.at[4])
+    staged = ((0, q, q_all, k, k_all), (1, g, g_all, v, v_all))
+    for n, ts, td, cs, cd in staged:
+        for i in range(dec):
+            mine = (home == z) & (z == i)
+            pl.when(jnp.logical_not(mine))(lambda: token_copy(n, ts, td, i).start())
+        pl.when(home == z)(lambda: token_own(n, ts, td).start())
+        if n == 0:
+            for j in range(1, dec):
+                bias_copy(j).start()
+            bias_own.start()
+        for j in range(1, enc):
+            cell_copy(n, cs, cd, j).start()
+        cell_own(n, cs, cd).start()
+    for n, ts, td, cs, cd in staged:
+        for i in range(dec):
+            mine = (home == z) & (z == i)
+            pl.when(jnp.logical_not(mine))(lambda: token_copy(n, ts, td, i).wait_send())
+            pl.when(jnp.logical_not(mine))(lambda: token_wait(n, ts, td, i).wait_recv())
+        pl.when(home == z)(lambda: token_own(n, ts, td).wait())
+        for j in range(1, enc):
+            cell_copy(n, cs, cd, j).wait_send()
+            cell_wait(n, cs, cd, j).wait_recv()
+        cell_own(n, cs, cd).wait()
+    for j in range(1, dec):
+        bias_copy(j).wait_send()
+        bias_wait(j).wait_recv()
+    bias_own.wait()
+
+
+def gather_kernel(
+    *refs
+):
+    enc, dec = lax.axis_size("enc"), lax.axis_size("dec")
+    per = enc // dec
+    e, z = lax.axis_index("enc"), lax.axis_index("dec")
+    t0, t1, c0, c1, o0, o1, d0, d1, tok_send, tok_recv, cell_send, cell_recv, local = refs
+    width = t0.shape[1]
+    tok, cells = o0.shape[0], d0.shape[0]
+    home, core = e // per, lax.rem(e, per)
+    slot = lambda x: lax.rem(x, per) * dec + x // per
+    greet_all()
+
+    def token_copy(n, src, dst, i):
+        return remote(
+            rows_of(src, i, tok), lanes(dst, home, width),
+            tok_send.at[n, i], tok_recv.at[n, home], (per * z + core, i),
+        )
+
+    def token_wait(n, src, dst, i):
+        return remote(
+            rows_of(src, 0, tok), lanes(dst, i, width),
+            tok_send.at[n, 0], tok_recv.at[n, i], (e, z),
+        )
+
+    def token_own(n, src, dst):
+        return pltpu.make_async_copy(rows_of(src, z, tok), lanes(dst, home, width), local.at[n])
+
+    def cell_copy(n, src, dst, j):
+        target = lax.rem(e + j, enc)
+        return remote(
+            rows_of(src, target, cells), lanes(dst, slot(e), width),
+            cell_send.at[n, j - 1], cell_recv.at[n, j - 1], (target, z),
+        )
+
+    def cell_wait(n, src, dst, j):
+        origin = lax.rem(e - j + enc, enc)
+        return remote(
+            rows_of(src, 0, cells), lanes(dst, slot(origin), width),
+            cell_send.at[n, j - 1], cell_recv.at[n, j - 1], (origin, z),
+        )
+
+    def cell_own(n, src, dst):
+        return pltpu.make_async_copy(
+            rows_of(src, e, cells), lanes(dst, slot(e), width), local.at[2 + n]
+        )
+
+    staged = ((0, t0, o0, c0, d0), (1, t1, o1, c1, d1))
+    for n, ts, td, cs, cd in staged:
+        for i in range(dec):
+            mine = (home == z) & (z == i)
+            pl.when(jnp.logical_not(mine))(lambda: token_copy(n, ts, td, i).start())
+        pl.when(home == z)(lambda: token_own(n, ts, td).start())
+        for j in range(1, enc):
+            cell_copy(n, cs, cd, j).start()
+        cell_own(n, cs, cd).start()
+    for n, ts, td, cs, cd in staged:
+        for i in range(dec):
+            mine = (home == z) & (z == i)
+            pl.when(jnp.logical_not(mine))(lambda: token_copy(n, ts, td, i).wait_send())
+            pl.when(jnp.logical_not(mine))(lambda: token_wait(n, ts, td, i).wait_recv())
+        pl.when(home == z)(lambda: token_own(n, ts, td).wait())
+        for j in range(1, enc):
+            cell_copy(n, cs, cd, j).wait_send()
+            cell_wait(n, cs, cd, j).wait_recv()
+        cell_own(n, cs, cd).wait()
+
+
+def scatter(q, k, bias, g, v):
+    enc, dec = lax.axis_size("enc"), lax.axis_size("dec")
+    width = k.shape[1] // (enc * dec)
+    bf = jnp.bfloat16
+    dma = pltpu.SemaphoreType.DMA
+    tokens = jax.ShapeDtypeStruct((dec * q.shape[0], width), bf)
+    cells = jax.ShapeDtypeStruct((enc * k.shape[0], width), bf)
+    return pl.pallas_call(
+        scatter_kernel,
+        out_shape=(
+            tokens, cells, jax.ShapeDtypeStruct((bias.shape[0], dec * bias.shape[1]), bf), tokens, cells
+        ),
+        in_specs=[pl.BlockSpec(memory_space=pl.ANY)] * 5,
+        out_specs=[pl.BlockSpec(memory_space=pl.ANY)] * 5,
+        scratch_shapes=[
+            dma((2, dec)), dma((2, dec)), dma((2, enc - 1)), dma((2, enc - 1)),
+            dma((dec - 1,)), dma((dec - 1,)), dma((5,)),
+        ],
+        compiler_params=pltpu.CompilerParams(collective_id=0, has_side_effects=True),
+        name="scatter_in",
+    )(q, k, bias, g, v)
+
+
+def gather(ctx, dq, dk, dv, tok, cells):
+    enc, dec = lax.axis_size("enc"), lax.axis_size("dec")
+    width = ctx.shape[1]
+    bf = jnp.bfloat16
+    dma = pltpu.SemaphoreType.DMA
+    token_out = jax.ShapeDtypeStruct((tok, dec * width), bf)
+    cell_out = jax.ShapeDtypeStruct((cells, enc * width), bf)
+    return pl.pallas_call(
+        gather_kernel,
+        out_shape=(token_out, token_out, cell_out, cell_out),
+        in_specs=[pl.BlockSpec(memory_space=pl.ANY)] * 4,
+        out_specs=[pl.BlockSpec(memory_space=pl.ANY)] * 4,
+        scratch_shapes=[
+            dma((2, dec)), dma((2, dec)), dma((2, enc - 1)), dma((2, enc - 1)), dma((4,)),
+        ],
+        compiler_params=pltpu.CompilerParams(collective_id=1, has_side_effects=True),
+        name="gather_out",
+    )(ctx, dq, dk, dv)
 
 
 def shared_head(q, g, k, v, bias, per, dec):
@@ -212,7 +447,7 @@
         )
         return total.astype(jnp.bfloat16)
 
-    bias = lax.dynamic_slice_in_dim(bias, place * rows, rows, 0)
+    bias = lax.dynamic_slice_in_dim(bias, place * rows, rows, 1)
     ctx, dq, dk, dv = attention(to_head(q), to_head(g), widen(k), widen(v), bias, jnp.float32)
     return from_head(ctx), from_head(dq), add_up(dk), add_up(dv)
 
@@ -246,7 +481,11 @@
         x = x.reshape(dec, per, own_cells, width).transpose(2, 1, 0, 3)
         return x.reshape(own_cells, full // dec)
 
-    bias = lax.all_gather(hidden_blocks(ref_blocks, ref_counts), "dec", tiled=True)
+    bias = hidden_blocks(ref_blocks, ref_counts, enc * own_cells // BLOCK)
+    if width % LANES == 0:
+        q, k, bias, g, v = scatter(queries, memory_keys, bias, out_grad, memory_values)
+        return gather(*attention(q, g, k, v, bias), tok, own_cells)
+    bias = lax.all_gather(bias, "dec", axis=1, tiled=True)
     q, g, k, v = token_in(queries), token_in(out_grad), cell_in(memory_keys), cell_in(memory_values)
     if width >= DH:
         ctx, dq, dk, dv = attention(q, g, k, v, bias)

time: 319 us -> 253 us (0.79)
  Pallas kernels: 119 us -> 238 us
  blocking collectives: 97.8 us -> 0 us
  waiting for transfers between devices: 44.6 us -> 0 us
  starting transfers between devices: 29 us -> 0 us
  local copies, waits for them, and re-layouts: 19.3 us -> 5.83 us
    pallas_call x0 -> x2, Pallas kernels: none -> 118 us  [the longest x1 73 us: scatter(): pl.pallas_call(scatter_kernel, out_shape=(tokens, cells, jax.ShapeDtypeSt...]
    all_to_all x5 -> x0, blocking collectives: 77.6 us -> none  [the longest x2 38 us: cell_out(): x = lax.all_to_all(x.reshape(enc, own_cells, width), 'enc', 0, 0)]
    all_to_all x7 -> x0, waiting for transfers between devices: 44.6 us -> none  [the longest x2 28.7 us: cell_in(): x = lax.all_to_all(x.reshape(enc, own_cells, width), 'enc', 0, 0)]
    all_to_all x7 -> x0, starting transfers between devices: 29 us -> none  [the longest x2 9.31 us: token_in(): x = lax.all_to_all(x, 'enc', 0, 0, axis_index_groups=groups)]
    all_gather x1 -> x0, blocking collectives: 20.2 us -> none  [body(): lax.all_gather(hidden_blocks(ref_blocks, ref_counts), 'dec', tiled=True)]
    reshape x6 -> x0, local copies, waits for them, and re-layouts: 8.41 us -> none  [the longest x2 4.12 us: cell_out(): return x.reshape(own_cells, full // dec)]
    transpose x4 -> x0, local copies, waits for them, and re-layouts: 5.34 us -> none  [the longest x2 3.57 us: cell_in(): x = x.reshape(own_cells, per, dec, width).transpose(2, 1, 0, 3)]
  transfers between devices with their start and end apart: 7 -> 0, of which waited for: 5 -> 0; matrix products, arithmetic and copies ran while one was open for 7% -> 0% of each run, Pallas kernels for 0% -> 0%
where the time goes in v2:
time: 253 us; the launch traced here: 251 us
  Pallas kernels  238 us (94%)
  other arithmetic  6.11 us (2%)
  local copies, waits for them, and re-layouts  5.83 us (2%)
    pallas_call x1, Pallas kernels, attention(): pl.pallas_call(functools.partial(attention_kernel, heads, chunk), grid=(t...  120 us
    pallas_call x1, Pallas kernels, scatter(): pl.pallas_call(scatter_kernel, out_shape=(tokens, cells, jax.ShapeDtypeSt...  73 us
    pallas_call x1, Pallas kernels, gather(): pl.pallas_call(gather_kernel, out_shape=(token_out, token_out, cell_out,...  45.2 us
    unnamed x8, local copies, waits for them, and re-layouts  5.83 us

profile of v2, /device:TPU:0, one launch (start us, length us, event | category | flops | bytes accessed | tf_op | source)
XLA Modules:
  0.0 250.5 jit_solution(11551804989565771092)
XLA Ops:
  0.7 0.7 select_bitcast_fusion
  1.4 0.1 fusion.2
  1.5 0.6 select_convert_fusion.bias
  2.1 4.7 %fusion.1.e_ref = bf16[4096,128]{1,0:T(8,128)(2,1)} fusion(s32[4096]{0:T(1024)S(1)} %get-tuple-element.22, s32[4096]{0:T(1024)S(1)} %get-tuple-element.23, pred[4096]{0:T(1024)(128)(4,1)S(1)} %fusion.5, pred[128]{0:T(512)(128)(4,1)S(1)} %iota_compare_fusion.3), kind=kLoop, calls=%fused_computation.2 | loop fusion | flops 2097152 | bytes 1085568 | tf_op jit(solution)/shard_map/convert_element_type | solution.py:144
  6.8 73.0 %scatter_in.1 = (bf16[2048,128]{1,0:T(8,128)(2,1)}, bf16[4096,128]{1,0:T(8,128)(2,1)}, bf16[32,2048]{1,0:T(8,128)(2,1)}, bf16[2048,128]{1,0:T(8,128)(2,1)}, bf16[4096,128]{1,0:T(8,128)(2,1)}) custom-call(bf16[512,512]{1,0:T(8,128)(2,1)} %q.1, bf16[512,4096]{1,0:T(8,128)(2,1)} %k.1, bf16[32,512]{1,0:T(8,128)(2,1)} %select_convert_fusion.bias, ...), custom_call_target="tpu_custom_call" | custom-call | tf_op jit(solution)/shard_map/scatter_in/pallas_call | solution.py:391
  79.7 119.8 %attention.1 = (bf16[2048,128]{1,0:T(8,128)(2,1)}, bf16[2048,128]{1,0:T(8,128)(2,1)}, bf16[4096,128]{1,0:T(8,128)(2,1)}, bf16[4096,128]{1,0:T(8,128)(2,1)}) custom-call(bf16[4096,128]{1,0:T(8,128)(2,1)} %get-tuple-element.13.k_ref, bf16[4096,128]{1,0:T(8,128)(2,1)} %get-tuple-element.14.v_ref, bf16[4096,128]{1,0:T(8,128)(2,1)} %fusion.1.e_ref, ...), custom_call_target="tpu_custom_call" | custom-call | tf_op jit(solution)/shard_map/attention/pallas_call | solution.py:156
  199.5 45.2 %gather_out.1 = (bf16[512,512]{1,0:T(8,128)(2,1)}, bf16[512,512]{1,0:T(8,128)(2,1)}, bf16[512,1024]{1,0:T(8,128)(2,1)}, bf16[512,1024]{1,0:T(8,128)(2,1)}) custom-call(bf16[2048,128]{1,0:T(8,128)(2,1)} %get-tuple-element.18.refs_0_, bf16[2048,128]{1,0:T(8,128)(2,1)} %get-tuple-element.19.refs_1_, bf16[4096,128]{1,0:T(8,128)(2,1)} %get-tuple-element.20.refs_2_, ...), custom_call_target="tpu_custom_call" | custom-call | tf_op jit(solution)/shard_map/gather_out/pallas_call | solution.py:414
  244.7 0.0 copy-start.1
  244.7 0.0 copy-start
  244.7 2.0 copy.14
  246.7 1.9 copy.15
  248.6 0.0 copy-done.1
  248.6 1.0 copy.16
  249.6 0.0 copy-done
  249.6 1.0 copy.17
  (3 shorter events, 0.0 us)
Async XLA Ops:
  244.7 3.9 %copy-start.1 = (bf16[512,1024]{1,0:T(8,128)(2,1)S(1)}, bf16[512,1024]{1,0:T(8,128)(2,1)}, u32[]{:S(2)}) copy-start(bf16[512,1024]{1,0:T(8,128)(2,1)} %get-tuple-element.30) | copy-start | bytes 3145732
  244.7 4.9 %copy-start = (bf16[512,1024]{1,0:T(8,128)(2,1)S(1)}, bf16[512,1024]{1,0:T(8,128)(2,1)}, u32[]{:S(2)}) copy-start(bf16[512,1024]{1,0:T(8,128)(2,1)} %get-tuple-element.31) | copy-start | bytes 3145732

commit v3 on v2

--- a/solution.py
+++ b/solution.py
@@ -144,10 +144,11 @@
     return ((block_ids == lane) | (lane >= LANES - 2)).astype(jnp.bfloat16)
 
 
-def attention(q, g, k, v, bias, grad_type=jnp.bfloat16, rows=256, chunk=512):
+def attention(q, g, k, v, bias, grad_type=jnp.bfloat16, rows=512, chunk=2048):
     tokens, width = q.shape
     cells = k.shape[0]
     heads = width // DH
+    chunk = min(chunk, cells)
     whole = lambda i: (0, 0)
     part = lambda i: (i, 0)
     cell_spec = pl.BlockSpec((cells, width), whole)
@@ -225,8 +226,8 @@
 
 
 def scatter_kernel(
-    q, k, bias, g, v, q_all, k_all, bias_all, g_all, v_all,
-    tok_send, tok_recv, cell_send, cell_recv, bias_send, bias_recv, local,
+    q, k, bias, g, v, q_all, k_all, bias_all, g_all, v_all, q_mid, g_mid,
+    mid_send, mid_recv, tok_send, tok_recv, cell_send, cell_recv, bias_send, bias_recv, local,
 ):
     enc, dec = lax.axis_size("enc"), lax.axis_size("dec")
     per = enc // dec
@@ -235,22 +236,51 @@
     tok, cells = q.shape[0], k.shape[0]
     home, core = e // per, lax.rem(e, per)
     slot = lambda x: z * enc + lax.rem(x, per) * dec + x // per
+    around = lambda x, d: lax.rem(x + d + dec, dec)
     greet_all()
 
-    def token_copy(n, src, dst, i):
-        return remote(
-            lanes(src, i, width), rows_of(dst, z, tok),
-            tok_send.at[n, i], tok_recv.at[n, z], (per * i + core, home),
-        )
-
-    def token_wait(n, src, dst, i):
-        return remote(
-            lanes(src, 0, width), rows_of(dst, i, tok),
-            tok_send.at[n, 0], tok_recv.at[n, i], (e, z),
-        )
-
-    def token_own(n, src, dst):
-        return pltpu.make_async_copy(lanes(src, home, width), rows_of(dst, z, tok), local.at[n])
+    def plane_copy(n, src, mid, d):
+        i = around(home, d)
+        return remote(
+            lanes(src, i, width), rows_of(mid, home, tok),
+            mid_send.at[n, d - 1], mid_recv.at[n, d - 1], (per * i + core, z),
+        )
+
+    def plane_wait(n, src, mid, d):
+        j = around(home, -d)
+        return remote(
+            lanes(src, 0, width), rows_of(mid, j, tok),
+            mid_send.at[n, d - 1], mid_recv.at[n, d - 1], (per * j + core, z),
+        )
+
+    def forward(n, src, mid, dst, d, act):
+        j = around(home, -d)
+        piece = lanes(src, home, width) if d == 0 else rows_of(mid, j, tok)
+        here = rows_of(dst, z, tok)
+
+        @pl.when(j == z)
+        def _():
+            act(pltpu.make_async_copy(piece, here, local.at[n]), False)
+
+        @pl.when(j != z)
+        def _():
+            act(remote(piece, here, tok_send.at[n, d], tok_recv.at[n, z], (e, j)), True)
+
+    def begin(copy, away):
+        copy.start()
+
+    def finish(copy, away):
+        if away:
+            copy.wait_send()
+        else:
+            copy.wait()
+
+    def token_wait(n, src, dst, t):
+        origin = around(z, -t)
+        return remote(
+            lanes(src, 0, width), rows_of(dst, origin, tok),
+            tok_send.at[n, 0], tok_recv.at[n, origin], (e, origin),
+        )
 
     def cell_copy(n, src, dst, j):
         target = lax.rem(e + j, enc)
@@ -272,41 +302,47 @@
         )
 
     def bias_copy(j):
-        target = lax.rem(z + j, dec)
-        return remote(
-            bias, lanes(bias_all, z, tok), bias_send.at[j - 1], bias_recv.at[j - 1], (e, target)
+        return remote(
+            bias, lanes(bias_all, z, tok), bias_send.at[j - 1], bias_recv.at[j - 1],
+            (e, around(z, j)),
         )
 
     def bias_wait(j):
-        origin = lax.rem(z - j + dec, dec)
-        return remote(
-            bias, lanes(bias_all, origin, tok), bias_send.at[j - 1], bias_recv.at[j - 1], (e, origin)
+        origin = around(z, -j)
+        return remote(
+            bias, lanes(bias_all, origin, tok), bias_send.at[j - 1], bias_recv.at[j - 1],
+            (e, origin),
         )
 
     bias_own = pltpu.make_async_copy(bias, lanes(bias_all, z, tok), local.at[4])
-    staged = ((0, q, q_all, k, k_all), (1, g, g_all, v, v_all))
-    for n, ts, td, cs, cd in staged:
-        for i in range(dec):
-            mine = (home == z) & (z == i)
-            pl.when(jnp.logical_not(mine))(lambda: token_copy(n, ts, td, i).start())
-        pl.when(home == z)(lambda: token_own(n, ts, td).start())
-        if n == 0:
-            for j in range(1, dec):
-                bias_copy(j).start()
-            bias_own.start()
+    staged = ((0, q, q_mid, q_all), (1, g, g_mid, g_all))
+    celled = ((0, k, k_all), (1, v, v_all))
+    for n, src, mid, dst in staged:
+        for d in range(1, dec):
+            plane_copy(n, src, mid, d).start()
+        forward(n, src, mid, dst, 0, begin)
+    for j in range(1, dec):
+        bias_copy(j).start()
+    bias_own.start()
+    for n, src, dst in celled:
         for j in range(1, enc):
-            cell_copy(n, cs, cd, j).start()
-        cell_own(n, cs, cd).start()
-    for n, ts, td, cs, cd in staged:
-        for i in range(dec):
-            mine = (home == z) & (z == i)
-            pl.when(jnp.logical_not(mine))(lambda: token_copy(n, ts, td, i).wait_send())
-            pl.when(jnp.logical_not(mine))(lambda: token_wait(n, ts, td, i).wait_recv())
-        pl.when(home == z)(lambda: token_own(n, ts, td).wait())
+            cell_copy(n, src, dst, j).start()
+        cell_own(n, src, dst).start()
+    for n, src, mid, dst in staged:
+        for d in range(1, dec):
+            plane_wait(n, src, mid, d).wait_recv()
+            forward(n, src, mid, dst, d, begin)
+    for n, src, mid, dst in staged:
+        for d in range(1, dec):
+            plane_copy(n, src, mid, d).wait_send()
+            token_wait(n, src, dst, d).wait_recv()
+        for d in range(dec):
+            forward(n, src, mid, dst, d, finish)
+    for n, src, dst in celled:
         for j in range(1, enc):
-            cell_copy(n, cs, cd, j).wait_send()
-            cell_wait(n, cs, cd, j).wait_recv()
-        cell_own(n, cs, cd).wait()
+            cell_copy(n, src, dst, j).wait_send()
+            cell_wait(n, src, dst, j).wait_recv()
+        cell_own(n, src, dst).wait()
     for j in range(1, dec):
         bias_copy(j).wait_send()
         bias_wait(j).wait_recv()
@@ -391,17 +427,19 @@
     return pl.pallas_call(
         scatter_kernel,
         out_shape=(
-            tokens, cells, jax.ShapeDtypeStruct((bias.shape[0], dec * bias.shape[1]), bf), tokens, cells
+            tokens, cells, jax.ShapeDtypeStruct((bias.shape[0], dec * bias.shape[1]), bf),
+            tokens, cells, tokens, tokens,
         ),
         in_specs=[pl.BlockSpec(memory_space=pl.ANY)] * 5,
-        out_specs=[pl.BlockSpec(memory_space=pl.ANY)] * 5,
+        out_specs=[pl.BlockSpec(memory_space=pl.ANY)] * 7,
         scratch_shapes=[
+            dma((2, dec - 1)), dma((2, dec - 1)),
             dma((2, dec)), dma((2, dec)), dma((2, enc - 1)), dma((2, enc - 1)),
             dma((dec - 1,)), dma((dec - 1,)), dma((5,)),
         ],
         compiler_params=pltpu.CompilerParams(collective_id=0, has_side_effects=True),
         name="scatter_in",
-    )(q, k, bias, g, v)
+    )(q, k, bias, g, v)[:5]
 
 
 def gather(ctx, dq, dk, dv, tok, cells):

time: 253 us -> 161 us (0.64)
  Pallas kernels: 238 us -> 146 us
    pallas_call x1, Pallas kernels: 120 us -> 64.4 us  [attention(): pl.pallas_call(functools.partial(attention_kernel, heads, chunk), grid=(t...]
    pallas_call x1, Pallas kernels: 73 us -> 42.2 us  [scatter(): pl.pallas_call(scatter_kernel, out_shape=(tokens, cells, jax.ShapeDtypeSt...]
    pallas_call x1, Pallas kernels: 45.2 us -> 39.5 us  [gather(): pl.pallas_call(gather_kernel, out_shape=(token_out, token_out, cell_out,...]
where the time goes in v3:
time: 161 us; the launch traced here: 159 us
  Pallas kernels  146 us (91%)
  other arithmetic  6.11 us (4%)
  local copies, waits for them, and re-layouts  5.83 us (4%)
    pallas_call x1, Pallas kernels, attention(): pl.pallas_call(functools.partial(attention_kernel, heads, chunk), grid=(t...  64.4 us
    pallas_call x1, Pallas kernels, scatter(): pl.pallas_call(scatter_kernel, out_shape=(tokens, cells, jax.ShapeDtypeSt...  42.2 us
    pallas_call x1, Pallas kernels, gather(): pl.pallas_call(gather_kernel, out_shape=(token_out, token_out, cell_out,...  39.5 us
    unnamed x8, local copies, waits for them, and re-layouts  5.83 us
    convert_element_type x1, other arithmetic, cell_marks(): return ((block_ids == lane) | (lane >= LANES - 2)).astype(jnp.bfloat16)  4.67 us

profile of v3, /device:TPU:0, one launch (start us, length us, event | category | flops | bytes accessed | tf_op | source)
XLA Modules:
  0.0 158.7 jit_solution(172572746109304931)
XLA Ops:
  0.7 0.7 select_bitcast_fusion
  1.4 0.1 fusion.2
  1.5 0.6 select_convert_fusion.bias
  2.1 4.7 %fusion.1.e_ref = bf16[4096,128]{1,0:T(8,128)(2,1)} fusion(s32[4096]{0:T(1024)S(1)} %get-tuple-element.22, s32[4096]{0:T(1024)S(1)} %get-tuple-element.23, pred[4096]{0:T(1024)(128)(4,1)S(1)} %fusion.5, pred[128]{0:T(512)(128)(4,1)S(1)} %iota_compare_fusion.3), kind=kLoop, calls=%fused_computation.2 | loop fusion | flops 2097152 | bytes 1085568 | tf_op jit(solution)/shard_map/convert_element_type | solution.py:144
  6.8 42.2 %scatter_in.1 = (bf16[2048,128]{1,0:T(8,128)(2,1)}, bf16[4096,128]{1,0:T(8,128)(2,1)}, bf16[32,2048]{1,0:T(8,128)(2,1)}, bf16[2048,128]{1,0:T(8,128)(2,1)}, bf16...) custom-call(bf16[512,512]{1,0:T(8,128)(2,1)} %q.1, bf16[512,4096]{1,0:T(8,128)(2,1)} %k.1, ...), custom_call_target="tpu_custom_call" | custom-call | tf_op jit(solution)/shard_map/scatter_in/pallas_call | solution.py:427
  49.0 64.4 %attention.1 = (bf16[2048,128]{1,0:T(8,128)(2,1)}, bf16[2048,128]{1,0:T(8,128)(2,1)}, bf16[4096,128]{1,0:T(8,128)(2,1)}, bf16[4096,128]{1,0:T(8,128)(2,1)}) custom-call(bf16[4096,128]{1,0:T(8,128)(2,1)} %get-tuple-element.13.k_ref, bf16[4096,128]{1,0:T(8,128)(2,1)} %get-tuple-element.14.v_ref, bf16[4096,128]{1,0:T(8,128)(2,1)} %fusion.1.e_ref, ...), custom_call_target="tpu_custom_call" | custom-call | tf_op jit(solution)/shard_map/attention/pallas_call | solution.py:157
  113.4 39.5 %gather_out.1 = (bf16[512,512]{1,0:T(8,128)(2,1)}, bf16[512,512]{1,0:T(8,128)(2,1)}, bf16[512,1024]{1,0:T(8,128)(2,1)}, bf16[512,1024]{1,0:T(8,128)(2,1)}) custom-call(bf16[2048,128]{1,0:T(8,128)(2,1)} %get-tuple-element.18.refs_0_, bf16[2048,128]{1,0:T(8,128)(2,1)} %get-tuple-element.19.refs_1_, bf16[4096,128]{1,0:T(8,128)(2,1)} %get-tuple-element.20.refs_2_, ...), custom_call_target="tpu_custom_call" | custom-call | tf_op jit(solution)/shard_map/gather_out/pallas_call | solution.py:452
  152.9 0.0 copy-start.1
  152.9 0.0 copy-start
  152.9 2.0 %copy.14 = bf16[512,512]{1,0:T(8,128)(2,1)} copy(bf16[512,512]{1,0:T(8,128)(2,1)} %get-tuple-element.28) | data formatting | bytes 1048576
  154.9 1.9 %copy.15 = bf16[512,512]{1,0:T(8,128)(2,1)} copy(bf16[512,512]{1,0:T(8,128)(2,1)} %get-tuple-element.29) | data formatting | bytes 1048576
  156.8 0.0 copy-done.1
  156.8 1.0 copy.16
  157.8 0.0 copy-done
  157.8 1.0 copy.17
  (3 shorter events, 0.0 us)
Async XLA Ops:
  152.9 3.9 %copy-start.1 = (bf16[512,1024]{1,0:T(8,128)(2,1)S(1)}, bf16[512,1024]{1,0:T(8,128)(2,1)}, u32[]{:S(2)}) copy-start(bf16[512,1024]{1,0:T(8,128)(2,1)} %get-tuple-element.30) | copy-start | bytes 3145732
  152.9 4.9 %copy-start = (bf16[512,1024]{1,0:T(8,128)(2,1)S(1)}, bf16[512,1024]{1,0:T(8,128)(2,1)}, u32[]{:S(2)}) copy-start(bf16[512,1024]{1,0:T(8,128)(2,1)} %get-tuple-element.31) | copy-start | bytes 3145732
